TPU v7x, 512 devices: a whole 4x4x16 slice. The times are simulated.
512 devices in a mesh: pix: 32 (over z_lo, y), mass: 16 (over z_hi, x, core).
Axes of the slice: x: 4, y: 4, z: 16 (z_hi: 2, z_lo: 8; z = z_hi * 8 + z_lo), core: 2. Of those that a mesh axis runs over, the one named last changes fastest.
Arguments:
- tiles: bfloat16 [32, 16, 16, 256, 256], P('pix', 'mass'), may hold values from 10 to 1000
- tile_pos: int32 [32, 16, 16], P('pix', 'mass'), may hold values from 0 to 255, as said below
- kept_tile_count: int32 [32, 16], P('pix', 'mass'), may hold values from 1 to 16, as said below
- loading: float32 [64, 65536], P('mass', 'pix'), may hold values from 0.006 to 6.5, as said below
- spectra: float32 [64, 131072], P('pix', 'mass'), may hold values from 0.006 to 6.5, as said below
Outputs:
- loading_new: float32 [64, 65536], P('mass', 'pix')
- spectra_new: float32 [64, 131072], P('pix', 'mass')
Inputs may be any that keep to these rules, and one draw needn't show every extreme that they name: `tile_pos`: on each device the 16 entries are distinct; entry q names tile row q // 32 and tile column q % 32 of the device's block. `kept_tile_count`: some device holds exactly 16 kept tiles. `loading`: every entry is positive. `spectra`: every entry is positive.
All inputs are finite; a program needn't handle non-finite values.
Results may differ from a plain program's by a relative error of at most 0.00065.
Values may be sent and summed in bfloat16 or wider, within the bound.
No kernel may reach another device: no remote copies, remote signals or barrier semaphores. Data moves between devices by JAX's collectives and lax.ppermute only.
A program may use at most 64 MiB of HBM per device.

v0:
```python
import jax
import jax.numpy as jnp
from jax import lax
from jax.sharding import PartitionSpec as P


def local(tiles, tile_pos, kept_tile_count, loading, spectra):
    largest_value = lax.Precision.HIGHEST
    stacked_tiles = tiles[0, 0]
    places = tile_pos[0, 0]
    kept_count = kept_tile_count[0, 0]
    slot_count = stacked_tiles.shape[0]
    tile_size = stacked_tiles.shape[1]
    mass_size = lax.axis_size("mass")
    rank_size = loading.shape[0] * mass_size
    pix_dev = loading.shape[1]
    bins_dev = spectra.shape[1]
    tile_rows = pix_dev // tile_size
    tile_cols = bins_dev // tile_size
    live_mask = (jnp.arange(slot_count) < kept_count).astype(jnp.float32)
    row_of = places // tile_cols
    col_of = places % tile_cols
    row_hot = (row_of[:, None] == jnp.arange(tile_rows)[None, :]).astype(jnp.float32) * live_mask[
        :, None
    ]
    column_onehot = (col_of[:, None] == jnp.arange(tile_cols)[None, :]).astype(
        jnp.float32
    ) * live_mask[:, None]
    whole_load = lax.all_gather(loading.astype(jnp.bfloat16), "mass", axis=0, tiled=True)
    gram_load = lax.psum(
        jnp.einsum("kp,jp->kj", whole_load, whole_load, preferred_element_type=jnp.float32), "pix"
    )
    selected_loading = jnp.take(whole_load.reshape(rank_size, tile_rows, tile_size), row_of, axis=1)
    spectra_matrix_product = jnp.einsum(
        "tco,com->ctm", selected_loading, stacked_tiles, preferred_element_type=jnp.float32
    )
    spectra_upper = jnp.einsum(
        "xo,xbm->bom", column_onehot, spectra_matrix_product, precision=largest_value
    ).reshape(rank_size, bins_dev)
    top_rows = lax.psum_scatter(spectra_upper, "pix", scatter_dimension=0, tiled=True)
    old_whole = lax.all_gather(spectra.astype(jnp.bfloat16), "pix", axis=0, tiled=True)
    spec_rows = spectra.shape[0]
    gram_rows = lax.dynamic_slice_in_dim(gram_load, lax.axis_index("pix") * spec_rows, spec_rows, 0)
    bottom_rows = jnp.dot(gram_rows, old_whole.astype(jnp.float32), precision=largest_value)
    spectra_new = spectra * top_rows / bottom_rows
    whole_spec = lax.all_gather(spectra_new.astype(jnp.bfloat16), "pix", axis=0, tiled=True)
    picked_spec = jnp.take(whole_spec.reshape(rank_size, tile_cols, tile_size), col_of, axis=1)
    load_product = jnp.einsum(
        "ksv,suv->sku", picked_spec, stacked_tiles, preferred_element_type=jnp.float32
    )
    load_top = jnp.einsum("sr,sku->kru", row_hot, load_product, precision=largest_value).reshape(
        rank_size, pix_dev
    )
    load_rows = loading.shape[0]
    gram_part = jnp.einsum("km,jm->kj", whole_spec, whole_spec, preferred_element_type=jnp.float32)
    top_mine = lax.psum_scatter(load_top, "mass", scatter_dimension=0, tiled=True)
    gram_spec = lax.psum(gram_part, "mass")
    gram_spec_rows = lax.dynamic_slice_in_dim(
        gram_spec, lax.axis_index("mass") * load_rows, load_rows, 0
    )
    load_bottom = jnp.dot(gram_spec_rows, whole_load.astype(jnp.float32), precision=largest_value)
    loading_new = loading * top_mine / load_bottom
    return (loading_new, spectra_new)


def solution(mesh):
    return jax.shard_map(
        local,
        mesh=mesh,
        in_specs=(
            P("pix", "mass", None, None, None),
            P("pix", "mass", None),
            P("pix", "mass"),
            P("mass", "pix"),
            P("pix", "mass"),
        ),
        out_specs=(P("mass", "pix"), P("pix", "mass")),
        check_vma=False,
    )
```

profile of v0, /device:TPU:1, one launch (start us, length us, event | category | flops | bytes accessed | tf_op | source)
XLA Modules:
  0.0 1191.5 jit_solution(17400756126792257851)
XLA Ops:
  7.2 1.6 convert_bitcast_fusion.1
  8.9 0.0 all-reduce.5.cloned.1.call-start
  9.6 0.8 convert_bitcast_fusion.2
  10.3 51.4 %all-gather = bf16[16,4,2048]{2,1,0:T(4,128)(2,1)S(1)} all-gather(bf16[1,4,2048]{2,1,0:T(4,128)(2,1)S(1)} %convert_bitcast_fusion.2), channel_id=1, replica_groups=mesh['pix'=32,'mass'=16] {'mass'}, dimensions={0}, use_global_device_ids=true | all-gather | bytes 278528 | tf_op jit(solution)/shard_map/all_gather | solution.py:29
  61.7 0.2 reshape.169
  62.0 0.7 fusion.29
  62.6 0.6 gather_fusion
  63.3 0.5 fusion.2
  63.8 2.3 fusion.6
  66.1 2.5 copy.19
  68.7 0.0 all-gather.8.cloned.1.call-start
  68.7 0.1 reshape.190
  68.8 1.3 dynamic-slice
  70.7 0.2 fusion.36
  70.9 203.7 %psum.14 = f32[64,64]{1,0:T(8,128)} all-reduce(f32[64,64]{1,0:T(8,128)S(1)} %fusion.36), channel_id=1, replica_groups=mesh['pix'=32,'mass'=16] {'pix'}, use_global_device_ids=true, to_apply=%region_1.2 | all-reduce | flops 4096 | bytes 32768 | tf_op jit(solution)/shard_map/psum | solution.py:30
  274.7 1.5 reshape.192
  276.1 399.9 %all-reduce.5.cloned.1.call-done = f32[64,8192]{1,0:T(8,128)} async-done(((f32[64,8192]{1,0:T(8,128)}), f32[64,8192]{1,0:T(8,128)}) %all-reduce.5.cloned.1.call-update) | async-done | bytes 2097168
  676.1 1.5 convolution_divide_fusion
  677.6 0.6 convert_bitcast_fusion
  678.3 221.1 %all-gather.8.cloned.1.call-done = bf16[32,2,8192]{2,1,0:T(2,128)(2,1)} async-done(((bf16[1,2,8192]{2,1,0:T(2,128)(2,1)}), bf16[32,2,8192]{2,1,0:T(2,128)(2,1)}) %all-gather.8.cloned.1.call-update) | async-done | bytes 1048592 | tf_op jit(solution)/shard_map/all_gather | solution.py:46
  899.5 1.7 reshape.171
  901.2 1.6 copy.17
  902.8 1.8 gather_fusion.1
  904.6 0.8 fusion
  905.4 1.3 fusion.4
  906.7 1.0 copy.20
  907.6 1.3 dynamic-slice.2
  909.6 1.5 reshape.194
  911.1 0.4 fusion.37
  911.5 131.7 %psum.15 = f32[64,64]{1,0:T(8,128)S(1)} all-reduce(f32[64,64]{1,0:T(8,128)S(1)} %fusion.37), channel_id=1, replica_groups=mesh['pix'=32,'mass'=16] {'mass'}, use_global_device_ids=true, to_apply=%region_3.4 | all-reduce | flops 4096 | bytes 32768 | tf_op jit(solution)/shard_map/psum | solution.py:57
  1043.2 140.1 %all-reduce.7.cloned.1.call-done = f32[64,2048]{1,0:T(8,128)} async-done(((f32[64,2048]{1,0:T(8,128)}), f32[64,2048]{1,0:T(8,128)}) %all-reduce.7.cloned.1.call-update) | async-done | bytes 524304
  1183.3 1.7 convolution_divide_fusion.1
  (21 shorter events, 0.3 us)
Async XLA Ops:
  7.2 56.1 %copy-start = (bf16[1,1,16,256,256]{4,3,2,1,0:T(8,128)(2,1)S(1)}, bf16[1,1,16,256,256]{4,3,2,1,0:T(8,128)(2,1)}, u32[]{:S(2)}) copy-start(bf16[1,1,16,256,256]{4,3,2,1,0:T(8,128)(2,1)} %param.5) | copy-start | bytes 6291460
  7.2 56.0 %copy-start.4 = (s32[1,1,16]{2,1,0:T(1,128)S(1)}, s32[1,1,16]{2,1,0:T(1,128)}, u32[]{:S(2)}) copy-start(s32[1,1,16]{2,1,0:T(1,128)} %param.6) | copy-start | bytes 196
  7.2 267.5 %all-gather.6.cloned.1.call-start = ((), (), s32[]{:S(2)}) async-start(), calls=%async_computation | async-start | bytes 1081344 | tf_op jit(solution)/shard_map/all_gather | solution.py:41
  8.9 667.2 %all-reduce.5.cloned.1.call-start = ((), (), s32[]{:S(2)}) async-start(), calls=%async_computation.2 | async-start | bytes 4194304
  68.7 607.4 %copy-start.1 = (f32[2,8192]{1,0:T(2,128)S(1)}, f32[2,8192]{1,0:T(2,128)}, u32[]{:S(2)}) copy-start(f32[2,8192]{1,0:T(2,128)} %param.9) | copy-start | bytes 196612
  68.7 830.8 %all-gather.8.cloned.1.call-start = ((), (), s32[]{:S(2)}) async-start(), calls=%async_computation.1 | async-start | bytes 1081344 | tf_op jit(solution)/shard_map/all_gather | solution.py:46
  677.6 225.2 %copy-start.2 = (f32[2,8192]{1,0:T(2,128)}, f32[2,8192]{1,0:T(2,128)S(1)}, u32[]{:S(2)}) copy-start(f32[2,8192]{1,0:T(2,128)S(1)} %convolution_divide_fusion) | copy-start | bytes 196612
  678.3 505.0 %all-reduce.7.cloned.1.call-start = ((), (), s32[]{:S(2)}) async-start(), calls=%async_computation.3 | async-start | bytes 1048576
  909.6 273.7 %copy-start.3 = (f32[4,2048]{1,0:T(4,128)S(1)}, f32[4,2048]{1,0:T(4,128)}, u32[]{:S(2)}) copy-start(f32[4,2048]{1,0:T(4,128)} %param.8) | copy-start | bytes 98308
Sparse Core Ops, SparseCore 0:
  10.7 205.9 all-gather.5
  219.6 456.4 all-reduce.4
  678.9 220.4 all-gather.7
  907.8 275.4 all-reduce.6
where the time goes:
time: 1190 us
  waiting for transfers between devices  761 us (64%)
  blocking collectives  387 us (33%)
  between operations  15.9 us (1%)
  local copies, waits for them, and re-layouts  15 us (1%)
    unnamed x6, waiting for transfers between devices  540 us
    all_gather x1, waiting for transfers between devices, local(): lax.all_gather(spectra_new.astype(jnp.bfloat16), 'pix', axis=0, tiled=True)  221 us
    psum x1, blocking collectives, local(): lax.psum(jnp.einsum('kp,jp->kj', whole_load, whole_load, preferred_elemen...  204 us
    psum x1, blocking collectives, local(): gram_spec = lax.psum(gram_part, 'mass')  132 us
    all_gather x1, blocking collectives, local(): lax.all_gather(loading.astype(jnp.bfloat16), 'mass', axis=0, tiled=True)  51.4 us
  transfers between devices with their start and end apart: 4, of which 3 were waited for; matrix products, arithmetic and copies ran while one was open for 1% of the time, Pallas kernels for 0%

commit v1 on v0

--- a/solution.py
+++ b/solution.py
@@ -43,7 +43,12 @@
     gram_rows = lax.dynamic_slice_in_dim(gram_load, lax.axis_index("pix") * spec_rows, spec_rows, 0)
     bottom_rows = jnp.dot(gram_rows, old_whole.astype(jnp.float32), precision=largest_value)
     spectra_new = spectra * top_rows / bottom_rows
-    whole_spec = lax.all_gather(spectra_new.astype(jnp.bfloat16), "pix", axis=0, tiled=True)
+    whole_spec = jnp.concatenate(
+        lax.all_to_all(
+            jnp.stack([spectra_new.astype(jnp.bfloat16)] * lax.axis_size("pix")), "pix", 0, 0
+        ),
+        axis=0,
+    )
     picked_spec = jnp.take(whole_spec.reshape(rank_size, tile_cols, tile_size), col_of, axis=1)
     load_product = jnp.einsum(
         "ksv,suv->sku", picked_spec, stacked_tiles, preferred_element_type=jnp.float32

time: 1190 us -> 1010 us (0.85)
  waiting for transfers between devices: 761 us -> 563 us
    all_gather x1 -> x0, waiting for transfers between devices: 221 us -> none  [local(): lax.all_gather(spectra_new.astype(jnp.bfloat16), 'pix', axis=0, tiled=True)]
    all_to_all x0 -> x1, waiting for transfers between devices: none -> 28.7 us  [local(): lax.all_to_all(jnp.stack([spectra_new.astype(jnp.bfloat16)] * lax.axis_si...]
    unnamed x6 -> x5, waiting for transfers between devices: 540 us -> 535 us
where the time goes in v1:
time: 1010 us
  waiting for transfers between devices  563 us (56%)
  blocking collectives  390 us (39%)
  local copies, waits for them, and re-layouts  18.4 us (2%)
  between operations  15.9 us (2%)
  matrix products  11.9 us (1%)
  starting transfers between devices  10.9 us (1%)
    unnamed x5, waiting for transfers between devices  535 us
    psum x1, blocking collectives, local(): lax.psum(jnp.einsum('kp,jp->kj', whole_load, whole_load, preferred_elemen...  204 us
    psum x1, blocking collectives, local(): gram_spec = lax.psum(gram_part, 'mass')  134 us
    all_gather x1, blocking collectives, local(): lax.all_gather(loading.astype(jnp.bfloat16), 'mass', axis=0, tiled=True)  51.4 us
    all_to_all x1, waiting for transfers between devices, local(): lax.all_to_all(jnp.stack([spectra_new.astype(jnp.bfloat16)] * lax.axis_si...  28.7 us
  transfers between devices with their start and end apart: 4, of which 3 were waited for; matrix products, arithmetic and copies ran while one was open for 1% of the time, Pallas kernels for 0%

profile of v1, /device:TPU:1, one launch (start us, length us, event | category | flops | bytes accessed | tf_op | source)
XLA Modules:
  0.0 1013.0 jit_solution(10682885696897774421)
XLA Ops:
  7.2 1.6 convert_bitcast_fusion
  8.9 0.0 all-reduce.5.cloned.1.call-start
  9.6 0.8 convert_bitcast_fusion.1
  10.3 51.4 %all-gather = bf16[16,4,2048]{2,1,0:T(4,128)(2,1)S(1)} all-gather(bf16[1,4,2048]{2,1,0:T(4,128)(2,1)S(1)} %convert_bitcast_fusion.1), channel_id=1, replica_groups=mesh['pix'=32,'mass'=16] {'mass'}, dimensions={0}, use_global_device_ids=true | all-gather | bytes 278528 | tf_op jit(solution)/shard_map/all_gather | solution.py:29
  61.7 0.2 reshape.171
  62.0 0.7 fusion.29
  62.6 0.6 gather_fusion
  63.3 0.5 fusion.2
  63.8 2.3 fusion.6
  66.1 2.5 copy.15
  68.7 0.1 reshape.192
  68.8 1.3 dynamic-slice
  70.7 0.2 fusion.37
  70.9 203.9 %psum.14 = f32[64,64]{1,0:T(8,128)S(1)} all-reduce(f32[64,64]{1,0:T(8,128)S(1)} %fusion.37), channel_id=1, replica_groups=mesh['pix'=32,'mass'=16] {'pix'}, use_global_device_ids=true, to_apply=%region_1.2 | all-reduce | flops 4096 | bytes 32768 | tf_op jit(solution)/shard_map/psum | solution.py:30
  274.8 1.5 reshape.194
  276.2 399.7 %all-reduce.5.cloned.1.call-done = f32[64,8192]{1,0:T(8,128)} async-done(((f32[64,8192]{1,0:T(8,128)}), f32[64,8192]{1,0:T(8,128)}) %all-reduce.5.cloned.1.call-update) | async-done | bytes 2097168
  675.9 2.1 fusion.36
  678.1 1.9 stack.2
  680.0 10.7 %all-to-all-start = ((bf16[32,2,8192]{2,1,0:T(2,128)(2,1)}), bf16[32,2,8192]{2,1,0:T(2,128)(2,1)S(1)}, u32[]{:S(2)}, u32[]{:S(2)}) async-start(bf16[32,2,8192]{2,1,0:T(2,128)(2,1)} %stack.2), calls=%async_computation | async-start | bytes 2097152 | tf_op jit(solution)/shard_map/all_to_all | solution.py:47
  690.8 28.7 %all-to-all-done = bf16[32,2,8192]{2,1,0:T(2,128)(2,1)S(1)} async-done(((bf16[32,2,8192]{2,1,0:T(2,128)(2,1)}), bf16[32,2,8192]{2,1,0:T(2,128)(2,1)S(1)}, u32[]{:S(2)}, u32[]{:S(2)}) %all-to-all-start) | async-done | bytes 1048608 | tf_op jit(solution)/shard_map/all_to_all | solution.py:47
  719.5 1.5 reshape_reshape.3
  721.0 2.8 copy.13
  723.8 2.6 gather_fusion.1
  726.4 1.8 fusion
  728.2 1.3 fusion.4
  729.4 1.0 copy.16
  730.4 1.3 dynamic-slice.2
  732.4 1.2 reshape.174
  733.6 2.0 fusion.38
  735.6 134.3 %psum.15 = f32[64,64]{1,0:T(8,128)S(1)} all-reduce(f32[64,64]{1,0:T(8,128)S(1)} %fusion.38), channel_id=1, replica_groups=mesh['pix'=32,'mass'=16] {'mass'}, use_global_device_ids=true, to_apply=%region_3.4 | all-reduce | flops 4096 | bytes 32768 | tf_op jit(solution)/shard_map/psum | solution.py:62
  869.8 134.9 %all-reduce.7.cloned.1.call-done = f32[64,2048]{1,0:T(8,128)} async-done(((f32[64,2048]{1,0:T(8,128)}), f32[64,2048]{1,0:T(8,128)}) %all-reduce.7.cloned.1.call-update) | async-done | bytes 524304
  1004.8 1.7 convolution_divide_fusion.1
  (18 shorter events, 0.2 us)
Async XLA Ops:
  7.2 56.1 %copy-start = (bf16[1,1,16,256,256]{4,3,2,1,0:T(8,128)(2,1)S(1)}, bf16[1,1,16,256,256]{4,3,2,1,0:T(8,128)(2,1)}, u32[]{:S(2)}) copy-start(bf16[1,1,16,256,256]{4,3,2,1,0:T(8,128)(2,1)} %param.5) | copy-start | bytes 6291460
  7.2 56.0 %copy-start.3 = (s32[1,1,16]{2,1,0:T(1,128)S(1)}, s32[1,1,16]{2,1,0:T(1,128)}, u32[]{:S(2)}) copy-start(s32[1,1,16]{2,1,0:T(1,128)} %param.6) | copy-start | bytes 196
  7.2 267.6 %all-gather.4.cloned.1.call-start = ((), (), s32[]{:S(2)}) async-start(), calls=%async_computation.1 | async-start | bytes 1081344 | tf_op jit(solution)/shard_map/all_gather | solution.py:41
  8.9 667.1 %all-reduce.5.cloned.1.call-start = ((), (), s32[]{:S(2)}) async-start(), calls=%async_computation.2 | async-start | bytes 4194304
  68.7 607.3 %copy-start.1 = (f32[2,8192]{1,0:T(2,128)S(1)}, f32[2,8192]{1,0:T(2,128)}, u32[]{:S(2)}) copy-start(f32[2,8192]{1,0:T(2,128)} %param.9) | copy-start | bytes 196612
  680.0 39.5 %all-to-all-start = ((bf16[32,2,8192]{2,1,0:T(2,128)(2,1)}), bf16[32,2,8192]{2,1,0:T(2,128)(2,1)S(1)}, u32[]{:S(2)}, u32[]{:S(2)}) async-start(bf16[32,2,8192]{2,1,0:T(2,128)(2,1)} %stack.2), calls=%async_computation | async-start | bytes 2097152 | tf_op jit(solution)/shard_map/all_to_all | solution.py:47
  690.7 314.1 %all-reduce.7.cloned.1.call-start = ((), (), s32[]{:S(2)}) async-start(), calls=%async_computation.3 | async-start | bytes 1048576
  732.3 272.5 %copy-start.2 = (f32[4,2048]{1,0:T(4,128)S(1)}, f32[4,2048]{1,0:T(4,128)}, u32[]{:S(2)}) copy-start(f32[4,2048]{1,0:T(4,128)} %param.8) | copy-start | bytes 98308
Sparse Core Ops, SparseCore 0:
  10.7 205.9 all-gather.3
  219.6 456.3 all-reduce.4
  730.5 274.2 all-reduce.6
